TPU v7x, 512 devices: a whole 4x4x16 slice. The times are simulated.
512 devices in a mesh: section: 16 (over x, z_hi), seq: 16 (over z_lo, y), mp: 2 (over core).
Axes of the slice: x: 4, y: 4, z: 16 (z_hi: 4, z_lo: 4; z = z_hi * 4 + z_lo), core: 2. Of those that a mesh axis runs over, the one named last changes fastest.
Arguments:
- query_rows: bfloat16 [16, 2048, 2048], P('section', 'seq', 'mp'), may hold values from -150 to 150
- key_row_matrix: bfloat16 [16, 2048, 1024], P('section', 'seq', 'mp'), may hold values from -13 to 13
- value_row_matrix: bfloat16 [16, 2048, 1024], P('section', 'seq', 'mp'), may hold values from -6 to 6
- out_grad: bfloat16 [16, 2048, 2048], P('section', 'seq', 'mp'), may hold values from -24 to 24
- w_query: bfloat16 [16, 5376, 2048], P('section', 'seq', 'mp'), may hold values from -0.078125 to 0.078125
- key_weight: bfloat16 [16, 5376, 1024], P('section', 'seq', 'mp'), may hold values from -0.078125 to 0.078125
- value_weight: bfloat16 [16, 5376, 1024], P('section', 'seq', 'mp'), may hold values from -0.078125 to 0.078125
- doc_ids: int32 [16, 2048], P('section'), may hold values from 0 to 5, never falling along the last dimension, each value on 1 to 682 neighbouring positions
Outputs:
- upstream: bfloat16 [16, 2048, 5376], P('section', None, ('seq', 'mp'))
All inputs are finite; a program needn't handle non-finite values.
Results may differ from a plain program's by a relative error of at most 0.0071.
Values may be sent and summed in bfloat16 or wider, within the bound.
A program may use at most 64 MiB of HBM per device.

v0:
```python
from functools import reduce
import math
import jax
import jax.numpy as jnp
from jax import lax
from jax.sharding import PartitionSpec as P

HEAD_WIDTH = 128
WINDOW = 512


def from_behind(shard, axis, by):
    size = lax.axis_size(axis)
    pairs = [(i, i + by) for i in range(size) if 0 <= i + by < size]
    return lax.ppermute(shard, axis, pairs)


def passed_along(block, axis, distance):
    devices = range(lax.axis_size(axis))
    route = [((i - distance) % len(devices), i) for i in devices]
    return lax.ppermute(block, axis, route)


def per_device(
    query_rows,
    key_row_matrix,
    value_row_matrix,
    out_grad,
    w_query,
    key_weight,
    value_weight,
    doc_ids,
):
    query_here = query_rows[0]
    key_here = key_row_matrix[0]
    value_here = value_row_matrix[0]
    grad_here = out_grad[0]
    documents = doc_ids[0]
    row_count = query_here.shape[0]
    kv_cols = key_here.shape[1]
    kv_heads = kv_cols // HEAD_WIDTH
    group_width = query_here.shape[1] // kv_cols
    scaling = 1.0 / math.sqrt(HEAD_WIDTH)
    seq_count = lax.axis_size("seq")
    seq_place = lax.axis_index("seq")
    reach_now = min((WINDOW - 1) // row_count + 1, seq_count - 1)
    kv_local = jnp.concatenate([key_here, value_here], axis=1)
    rim_blocks = [from_behind(kv_local, "seq", distance) for distance in range(reach_now, 0, -1)]
    kv_blocks = rim_blocks + [kv_local]
    block_total = len(kv_blocks)
    span_rows = block_total * row_count
    first_row = seq_place * row_count
    padded_docs = jnp.concatenate([jnp.full((reach_now * row_count,), -1, jnp.int32), documents])
    key_docs = lax.dynamic_slice_in_dim(padded_docs, first_row, span_rows, 0)
    query_docs = lax.dynamic_slice_in_dim(documents, first_row, row_count, 0)
    query_pos = first_row + jnp.arange(row_count, dtype=jnp.int32)
    key_pos = first_row - reach_now * row_count + jnp.arange(span_rows, dtype=jnp.int32)
    offset = query_pos[:, None] - key_pos[None, :]
    allowed = (query_docs[:, None] == key_docs[None, :]) & (offset >= 0) & (offset < WINDOW)
    query_split = query_here.reshape(row_count, kv_heads, group_width, HEAD_WIDTH)
    grad_split = grad_here.reshape(row_count, kv_heads, group_width, HEAD_WIDTH)
    block_masks = [
        allowed[:, block_index * row_count : (block_index + 1) * row_count]
        for block_index in range(block_total)
    ]
    block_keys = [
        kv_block[:, :kv_cols].reshape(row_count, kv_heads, HEAD_WIDTH) for kv_block in kv_blocks
    ]
    block_values = [
        kv_block[:, kv_cols:].reshape(row_count, kv_heads, HEAD_WIDTH) for kv_block in kv_blocks
    ]

    def score_pair(key_block, mask_now):

        def make_fn():
            product = (
                jnp.einsum(
                    "igrd,jgd->grij", query_split, key_block, preferred_element_type=jnp.float32
                )
                * scaling
            )
            return jnp.where(mask_now[None, None], product, -jnp.inf)

        def empty_fn():
            return jnp.full((kv_heads, group_width, row_count, row_count), -jnp.inf, jnp.float32)

        return (make_fn, empty_fn)

    scores = []
    for block_index in range(block_total):
        make_fn, empty_fn = score_pair(block_keys[block_index], block_masks[block_index])
        scores.append(make_fn())
    row_max = reduce(
        jnp.maximum, [jnp.max(score_now, axis=-1, keepdims=True) for score_now in scores]
    )
    raised = [jnp.exp(score_now - row_max) for score_now in scores]
    row_total = reduce(
        jnp.add, [jnp.sum(raised_now, axis=-1, keepdims=True) for raised_now in raised]
    )
    weights_full = [raised_now / row_total for raised_now in raised]
    weights_half = [weight_now.astype(jnp.bfloat16) for weight_now in weights_full]

    def value_pair(weight_half, value_block):

        def make_fn():
            return jnp.einsum(
                "grij,jgd->igrd", weight_half, value_block, preferred_element_type=jnp.float32
            )

        def empty_fn():
            return jnp.zeros((row_count, kv_heads, group_width, HEAD_WIDTH), jnp.float32)

        return (make_fn, empty_fn)

    attended_terms = []
    for block_index in range(block_total):
        make_fn, empty_fn = value_pair(weights_half[block_index], block_values[block_index])
        attended_terms.append(make_fn())
    attended = reduce(jnp.add, attended_terms)
    delta_row = jnp.transpose(
        jnp.sum(grad_split.astype(jnp.float32) * attended, axis=-1), (1, 2, 0)
    )

    def grad_pair(weight_full, weight_half, key_block, value_block):

        def make_fn():
            grad_weights = jnp.einsum(
                "igrd,jgd->grij", grad_split, value_block, preferred_element_type=jnp.float32
            )
            grad_scores = (weight_full * (grad_weights - delta_row[..., None])).astype(jnp.bfloat16)
            query_term = jnp.einsum(
                "grij,jgd->igrd", grad_scores, key_block, preferred_element_type=jnp.float32
            )
            key_term = (
                jnp.einsum(
                    "grij,igrd->jgd", grad_scores, query_split, preferred_element_type=jnp.float32
                )
                * scaling
            )
            value_term = jnp.einsum(
                "grij,igrd->jgd", weight_half, grad_split, preferred_element_type=jnp.float32
            )
            kv_term = jnp.concatenate(
                [key_term.reshape(row_count, kv_cols), value_term.reshape(row_count, kv_cols)],
                axis=1,
            )
            return (query_term, kv_term)

        def empty_fn():
            return (
                jnp.zeros((row_count, kv_heads, group_width, HEAD_WIDTH), jnp.float32),
                jnp.zeros((row_count, 2 * kv_cols), jnp.float32),
            )

        return (make_fn, empty_fn)

    query_terms = []
    kv_terms = []
    for block_index in range(block_total):
        make_fn, empty_fn = grad_pair(
            weights_full[block_index],
            weights_half[block_index],
            block_keys[block_index],
            block_values[block_index],
        )
        query_term, kv_term = make_fn()
        query_terms.append(query_term)
        kv_terms.append(kv_term)
    query_grad = (
        (reduce(jnp.add, query_terms) * scaling)
        .astype(jnp.bfloat16)
        .reshape(row_count, kv_heads * group_width * HEAD_WIDTH)
    )
    kv_total = kv_terms[-1]
    for distance in range(1, reach_now + 1):
        kv_total = kv_total + from_behind(kv_terms[reach_now - distance], "seq", -distance)
    grad_matrix = jnp.concatenate([query_grad, kv_total.astype(jnp.bfloat16)], axis=1)
    weights_all = jnp.concatenate([w_query[0], key_weight[0], value_weight[0]], axis=1)
    partial_grad = lax.dot_general(
        lax.all_gather(grad_matrix, "seq", axis=0, tiled=True),
        weights_all,
        (((1,), (1,)), ((), ())),
        preferred_element_type=jnp.float32,
    )
    summed = lax.psum_scatter(partial_grad, "mp", scatter_dimension=1, tiled=True)
    grad_input = summed.astype(jnp.bfloat16)
    upstream = passed_along(grad_input, "section", -1)
    return upstream[None]


def solution(mesh):
    placed = (
        P("section", "seq", "mp"),
        P("section", "seq", "mp"),
        P("section", "seq", "mp"),
        P("section", "seq", "mp"),
        P("section", "seq", "mp"),
        P("section", "seq", "mp"),
        P("section", "seq", "mp"),
        P("section", None),
    )
    return jax.shard_map(
        per_device,
        mesh=mesh,
        in_specs=placed,
        out_specs=P("section", None, ("seq", "mp")),
        check_vma=False,
    )
```

profile of v0, /device:TPU:8, one launch (start us, length us, event | category | flops | bytes accessed | tf_op | source)
XLA Modules:
  0.0 336.0 jit_solution(13602698483485576235)
XLA Ops:
  6.5 1.1 copy.60
  7.6 1.0 copy.61
  8.7 3.5 %collective-permute-start.3 = (bf16[128,1024]{0,1:T(8,128)(2,1)S(1)}, bf16[128,1024]{0,1:T(8,128)(2,1)S(1)}, u32[]{:S(2)}, u32[]{:S(2)}) collective-permute-start(bf16[128,1024]{0,1:T(8,128)(2,1)S(1)} %pad_maximum_fusion.5), channel_id=1, source_target_pairs={{0,2},{2,4},{4,6},{6,8},{8,10},{10,12},{12,14},{14,16},{16,18},{18... | collective-permute-start | bytes 786440 | tf_op jit(solution)/shard_map/ppermute | solution.py:15
  12.2 4.2 %collective-permute-start.2 = (bf16[128,1024]{0,1:T(8,128)(2,1)S(1)}, bf16[128,1024]{0,1:T(8,128)(2,1)S(1)}, u32[]{:S(2)}, u32[]{:S(2)}) collective-permute-start(bf16[128,1024]{0,1:T(8,128)(2,1)S(1)} %pad_maximum_fusion.5), channel_id=1, source_target_pairs={{0,4},{2,6},{4,8},{6,10},{8,12},{10,14},{12,16},{14,18},{16,20},{1... | collective-permute-start | bytes 786440 | tf_op jit(solution)/shard_map/ppermute | solution.py:15
  16.4 4.3 %collective-permute-start.1 = (bf16[128,1024]{0,1:T(8,128)(2,1)S(1)}, bf16[128,1024]{0,1:T(8,128)(2,1)S(1)}, u32[]{:S(2)}, u32[]{:S(2)}) collective-permute-start(bf16[128,1024]{0,1:T(8,128)(2,1)S(1)} %pad_maximum_fusion.5), channel_id=1, source_target_pairs={{0,6},{2,8},{4,10},{6,12},{8,14},{10,16},{12,18},{14,20},{16,22},{... | collective-permute-start | bytes 786440 | tf_op jit(solution)/shard_map/ppermute | solution.py:15
  20.7 3.8 %collective-permute-start = (bf16[128,1024]{0,1:T(8,128)(2,1)S(1)}, bf16[128,1024]{0,1:T(8,128)(2,1)S(1)}, u32[]{:S(2)}, u32[]{:S(2)}) collective-permute-start(bf16[128,1024]{0,1:T(8,128)(2,1)S(1)} %pad_maximum_fusion.5), channel_id=1, source_target_pairs={{0,8},{2,10},{4,12},{6,14},{8,16},{10,18},{12,20},{14,22},{16,24},... | collective-permute-start | bytes 786440 | tf_op jit(solution)/shard_map/ppermute | solution.py:15
  24.6 0.7 dynamic-slice_bitcast_fusion
  25.2 0.8 pad_dynamic-slice_fusion
  26.0 0.2 fusion.63
  26.3 0.9 reshape_squeeze.13
  27.2 0.9 reshape_squeeze.15
  28.1 0.1 copy.144
  28.3 1.1 copy.189
  29.4 0.2 copy.72
  29.6 0.3 fusion.77
  29.9 1.5 collective-permute-done
  31.4 0.3 fusion.80
  31.7 0.3 fusion.81
  32.0 0.3 fusion.79
  32.4 0.3 fusion.78
  32.7 0.5 fusion.55
  33.2 0.5 fusion.67
  33.6 0.2 fusion.91
  33.9 0.2 fusion.82
  34.1 0.2 fusion.90
  34.3 0.2 fusion.83
  34.5 0.2 fusion.89
  34.8 0.2 fusion.84
  35.0 0.2 fusion.88
  35.2 0.3 convolution_bitcast_fusion.1
  35.5 0.3 fusion.42
  35.8 0.3 fusion.39
  36.1 0.3 fusion.38
  36.4 0.3 fusion.37
  36.7 0.2 fusion.36
  36.9 0.3 fusion.40
  37.2 0.2 fusion.92
  37.4 0.2 fusion.44
  37.6 0.2 fusion.87
  37.9 0.2 fusion.46
  38.1 0.2 fusion.85
  38.3 0.2 fusion.45
  38.5 0.2 fusion.86
  38.8 0.2 fusion.47
  39.0 0.2 convolution_bitcast_fusion
  39.3 1.3 collective-permute-start.5
  40.6 1.3 collective-permute-start.6
  41.9 1.9 collective-permute-start.4
  43.9 1.3 collective-permute-start.7
  45.2 0.2 fusion.43
  45.5 0.3 fusion.41
  45.8 13.9 %collective-permute-done.5 = f32[128,1024]{0,1:T(8,128)S(1)} collective-permute-done((f32[128,1024]{0,1:T(8,128)S(1)}, f32[128,1024]{0,1:T(8,128)S(1)}, u32[]{:S(2)}, u32[]{:S(2)}) %collective-permute-start.5) | collective-permute-done | bytes 524320 | tf_op jit(solution)/shard_map/ppermute | solution.py:15
  59.7 14.0 %collective-permute-done.6 = f32[128,1024]{0,1:T(8,128)S(1)} collective-permute-done((f32[128,1024]{0,1:T(8,128)S(1)}, f32[128,1024]{0,1:T(8,128)S(1)}, u32[]{:S(2)}, u32[]{:S(2)}) %collective-permute-start.6) | collective-permute-done | bytes 524320 | tf_op jit(solution)/shard_map/ppermute | solution.py:15
  73.6 8.8 %collective-permute-done.7 = f32[128,1024]{0,1:T(8,128)S(1)} collective-permute-done((f32[128,1024]{0,1:T(8,128)S(1)}, f32[128,1024]{0,1:T(8,128)S(1)}, u32[]{:S(2)}, u32[]{:S(2)}) %collective-permute-start.7) | collective-permute-done | bytes 524320 | tf_op jit(solution)/shard_map/ppermute | solution.py:15
  82.5 0.1 fusion.51
  82.6 0.8 pad_maximum_fusion.4
  83.5 0.0 reduce-scatter.2.cloned.1.call-start
  83.5 145.0 %all-gather.2.cloned.1.call-done = bf16[2048,2048]{0,1:T(8,128)(2,1)} async-done(((bf16[128,2048]{0,1:T(8,128)(2,1)}), bf16[2048,2048]{0,1:T(8,128)(2,1)}) %all-gather.2.cloned.1.call-update) | async-done | bytes 8388624 | tf_op jit(solution)/shard_map/all_gather | solution.py:180
  228.5 8.0 %fusion = f32[2048,336]{0,1:T(8,128)} fusion(bf16[2048,2048]{0,1:T(8,128)(2,1)} %all-gather.2.cloned.1.call-done, bf16[336,512]{1,0:T(8,128)(2,1)S(1)} %bitcast.386, bf16[336,512]{1,0:T(8,128)(2,1)S(1)} %bitcast.387, bf16[336,1024]{1,0:T(8,128)(2,1)S(1)} %bitcast.385), kind=kOutput, calls=%fused_computation | convolution fusion | flops 2822701056 | bytes 12517376 | tf_op jit(solution)/shard_map/dot_general | solution.py:179
  236.5 20.4 %reduce-scatter.2.cloned.1.call-done = f32[2048,168]{0,1:T(8,128)} async-done(((f32[2048,336]{0,1:T(8,128)}), f32[2048,168]{0,1:T(8,128)}) %reduce-scatter.2.cloned.1.call-update) | async-done | bytes 1376272 | tf_op jit(solution)/shard_map/reduce_scatter | solution.py:185
  257.0 1.4 convert_element_type.55
  258.4 10.5 %collective-permute-start.8 = (bf16[2048,168]{0,1:T(8,128)(2,1)S(1)}, bf16[2048,168]{0,1:T(8,128)(2,1)S(1)}, u32[]{:S(2)}, u32[]{:S(2)}) collective-permute-start(bf16[2048,168]{0,1:T(8,128)(2,1)S(1)} %convert_element_type.55), channel_id=1, source_target_pairs={{32,0},{64,32},{96,64},{128,96},{160,128},{192,160},{224,192},{256... | collective-permute-start | bytes 2064392 | tf_op jit(solution)/shard_map/ppermute | solution.py:21
  268.9 59.4 %collective-permute-done.8 = bf16[2048,168]{0,1:T(8,128)(2,1)S(1)} collective-permute-done((bf16[2048,168]{0,1:T(8,128)(2,1)S(1)}, bf16[2048,168]{0,1:T(8,128)(2,1)S(1)}, u32[]{:S(2)}, u32[]{:S(2)}) %collective-permute-start.8) | collective-permute-done | bytes 688160 | tf_op jit(solution)/shard_map/ppermute | solution.py:21
  328.3 0.8 copy.195
  (28 shorter events, 0.3 us)
Async XLA Ops:
  6.5 22.9 %copy-start = (bf16[1,128,1024]{2,1,0:T(8,128)(2,1)S(1)}, bf16[1,128,1024]{2,1,0:T(8,128)(2,1)}, u32[]{:S(2)}) copy-start(bf16[1,128,1024]{2,1,0:T(8,128)(2,1)} %param.11) | copy-start | bytes 786436
  6.5 222.0 %all-gather.2.cloned.1.call-start = ((), (), s32[]{:S(2)}) async-start(), calls=%async_computation.1 | async-start | bytes 8912896 | tf_op jit(solution)/shard_map/all_gather | solution.py:180
  8.7 23.7 %collective-permute-start.3 = (bf16[128,1024]{0,1:T(8,128)(2,1)S(1)}, bf16[128,1024]{0,1:T(8,128)(2,1)S(1)}, u32[]{:S(2)}, u32[]{:S(2)}) collective-permute-start(bf16[128,1024]{0,1:T(8,128)(2,1)S(1)} %pad_maximum_fusion.5), channel_id=1, source_target_pairs={{0,2},{2,4},{4,6},{6,8},{8,10},{10,12},{12,14},{14,16},{16,18},{18... | collective-permute-start | bytes 786440 | tf_op jit(solution)/shard_map/ppermute | solution.py:15
  12.2 19.8 %collective-permute-start.2 = (bf16[128,1024]{0,1:T(8,128)(2,1)S(1)}, bf16[128,1024]{0,1:T(8,128)(2,1)S(1)}, u32[]{:S(2)}, u32[]{:S(2)}) collective-permute-start(bf16[128,1024]{0,1:T(8,128)(2,1)S(1)} %pad_maximum_fusion.5), channel_id=1, source_target_pairs={{0,4},{2,6},{4,8},{6,10},{8,12},{10,14},{12,16},{14,18},{16,20},{1... | collective-permute-start | bytes 786440 | tf_op jit(solution)/shard_map/ppermute | solution.py:15
  16.4 15.3 %collective-permute-start.1 = (bf16[128,1024]{0,1:T(8,128)(2,1)S(1)}, bf16[128,1024]{0,1:T(8,128)(2,1)S(1)}, u32[]{:S(2)}, u32[]{:S(2)}) collective-permute-start(bf16[128,1024]{0,1:T(8,128)(2,1)S(1)} %pad_maximum_fusion.5), channel_id=1, source_target_pairs={{0,6},{2,8},{4,10},{6,12},{8,14},{10,16},{12,18},{14,20},{16,22},{... | collective-permute-start | bytes 786440 | tf_op jit(solution)/shard_map/ppermute | solution.py:15
  20.7 10.6 %collective-permute-start = (bf16[128,1024]{0,1:T(8,128)(2,1)S(1)}, bf16[128,1024]{0,1:T(8,128)(2,1)S(1)}, u32[]{:S(2)}, u32[]{:S(2)}) collective-permute-start(bf16[128,1024]{0,1:T(8,128)(2,1)S(1)} %pad_maximum_fusion.5), channel_id=1, source_target_pairs={{0,8},{2,10},{4,12},{6,14},{8,16},{10,18},{12,20},{14,22},{16,24},... | collective-permute-start | bytes 786440 | tf_op jit(solution)/shard_map/ppermute | solution.py:15
  39.3 20.4 %collective-permute-start.5 = (f32[128,1024]{0,1:T(8,128)S(1)}, f32[128,1024]{0,1:T(8,128)S(1)}, u32[]{:S(2)}, u32[]{:S(2)}) collective-permute-start(f32[128,1024]{0,1:T(8,128)S(1)} %pad_maximum_fusion.1), channel_id=1, source_target_pairs={{4,0},{6,2},{8,4},{10,6},{12,8},{14,10},{16,12},{18,14},{20,16},{2... | collective-permute-start | bytes 1572872 | tf_op jit(solution)/shard_map/ppermute | solution.py:15
  40.6 33.0 %collective-permute-start.6 = (f32[128,1024]{0,1:T(8,128)S(1)}, f32[128,1024]{0,1:T(8,128)S(1)}, u32[]{:S(2)}, u32[]{:S(2)}) collective-permute-start(f32[128,1024]{0,1:T(8,128)S(1)} %pad_maximum_fusion.2), channel_id=1, source_target_pairs={{6,0},{8,2},{10,4},{12,6},{14,8},{16,10},{18,12},{20,14},{22,16},{... | collective-permute-start | bytes 1572872 | tf_op jit(solution)/shard_map/ppermute | solution.py:15
  41.9 31.7 %collective-permute-start.4 = (f32[128,1024]{0,1:T(8,128)S(1)}, f32[128,1024]{0,1:T(8,128)S(1)}, u32[]{:S(2)}, u32[]{:S(2)}) collective-permute-start(f32[128,1024]{0,1:T(8,128)S(1)} %pad_maximum_fusion), channel_id=1, source_target_pairs={{2,0},{4,2},{6,4},{8,6},{10,8},{12,10},{14,12},{16,14},{18,16},{20... | collective-permute-start | bytes 1572872 | tf_op jit(solution)/shard_map/ppermute | solution.py:15
  43.9 38.6 %collective-permute-start.7 = (f32[128,1024]{0,1:T(8,128)S(1)}, f32[128,1024]{0,1:T(8,128)S(1)}, u32[]{:S(2)}, u32[]{:S(2)}) collective-permute-start(f32[128,1024]{0,1:T(8,128)S(1)} %pad_maximum_fusion.3), channel_id=1, source_target_pairs={{8,0},{10,2},{12,4},{14,6},{16,8},{18,10},{20,12},{22,14},{24,16},... | collective-permute-start | bytes 1572872 | tf_op jit(solution)/shard_map/ppermute | solution.py:15
  45.7 182.8 %copy-start.1 = (bf16[1,336,1024]{2,1,0:T(8,128)(2,1)S(1)}, bf16[1,336,1024]{2,1,0:T(8,128)(2,1)}, u32[]{:S(2)}) copy-start(bf16[1,336,1024]{2,1,0:T(8,128)(2,1)} %param.12) | copy-start | bytes 2064388
  45.7 182.8 %copy-start.2 = (bf16[1,336,512]{2,1,0:T(8,128)(2,1)S(1)}, bf16[1,336,512]{2,1,0:T(8,128)(2,1)}, u32[]{:S(2)}) copy-start(bf16[1,336,512]{2,1,0:T(8,128)(2,1)} %param.14) | copy-start | bytes 1032196
  45.8 182.7 %copy-start.3 = (bf16[1,336,512]{2,1,0:T(8,128)(2,1)S(1)}, bf16[1,336,512]{2,1,0:T(8,128)(2,1)}, u32[]{:S(2)}) copy-start(bf16[1,336,512]{2,1,0:T(8,128)(2,1)} %param.13) | copy-start | bytes 1032196
  83.5 173.5 %reduce-scatter.2.cloned.1.call-start = ((), (), s32[]{:S(2)}) async-start(), calls=%async_computation.2 | async-start | bytes 4128768 | tf_op jit(solution)/shard_map/reduce_scatter | solution.py:185
  258.4 69.9 %collective-permute-start.8 = (bf16[2048,168]{0,1:T(8,128)(2,1)S(1)}, bf16[2048,168]{0,1:T(8,128)(2,1)S(1)}, u32[]{:S(2)}, u32[]{:S(2)}) collective-permute-start(bf16[2048,168]{0,1:T(8,128)(2,1)S(1)} %convert_element_type.55), channel_id=1, source_target_pairs={{32,0},{64,32},{96,64},{128,96},{160,128},{192,160},{224,192},{256... | collective-permute-start | bytes 2064392 | tf_op jit(solution)/shard_map/ppermute | solution.py:21
Sparse Core Ops, SparseCore 0:
  83.6 144.8 all-gather.1
  236.7 20.2 reduce-scatter.1
where the time goes:
time: 337 us; the launch traced here: 336 us
  waiting for transfers between devices  263 us (78%)
  starting transfers between devices  32.2 us (10%)
  matrix products  15.4 us (5%)
  between operations  13.9 us (4%)
  local copies, waits for them, and re-layouts  7.01 us (2%)
  other arithmetic  4.5 us (1%)
    all_gather x1, waiting for transfers between devices, per_device(): lax.all_gather(grad_matrix, 'seq', axis=0, tiled=True)  145 us
    ppermute x1, waiting for transfers between devices, passed_along(): return lax.ppermute(block, axis, route)  59.4 us
    ppermute x8, waiting for transfers between devices, from_behind(): return lax.ppermute(shard, axis, pairs)  38.2 us
    ppermute x8, starting transfers between devices, from_behind(): return lax.ppermute(shard, axis, pairs)  21.6 us
    reduce_scatter x1, waiting for transfers between devices, per_device(): lax.psum_scatter(partial_grad, 'mp', scatter_dimension=1, tiled=True)  20.4 us
    ppermute x1, starting transfers between devices, passed_along(): return lax.ppermute(block, axis, route)  10.5 us
    dot_general x1, matrix products, per_device(): lax.dot_general(lax.all_gather(grad_matrix, 'seq', axis=0, tiled=True), w...  8.02 us
  transfers between devices with their start and end apart: 11, of which 7 were waited for; matrix products, arithmetic and copies ran while one was open for 2% of the time, Pallas kernels for 0%

commit v1 on v0

--- a/solution.py
+++ b/solution.py
@@ -7,6 +7,13 @@
 
 HEAD_WIDTH = 128
 WINDOW = 512
+
+
+def all_by_exchange(array, mesh_axis, dim):
+    size = lax.axis_size(mesh_axis)
+    blocks = jnp.stack([array for _ in range(size)])
+    blocks = lax.all_to_all(blocks, mesh_axis, split_axis=0, concat_axis=0)
+    return jnp.concatenate(blocks, axis=dim)
 
 
 def from_behind(shard, axis, by):
@@ -177,7 +184,7 @@
     grad_matrix = jnp.concatenate([query_grad, kv_total.astype(jnp.bfloat16)], axis=1)
     weights_all = jnp.concatenate([w_query[0], key_weight[0], value_weight[0]], axis=1)
     partial_grad = lax.dot_general(
-        lax.all_gather(grad_matrix, "seq", axis=0, tiled=True),
+        all_by_exchange(grad_matrix, "seq", 0),
         weights_all,
         (((1,), (1,)), ((), ())),
         preferred_element_type=jnp.float32,

time: 337 us -> 389 us (1.15)
  blocking collectives: 0 us -> 197 us
  waiting for transfers between devices: 263 us -> 121 us
    all_to_all x0 -> x1, blocking collectives: none -> 197 us  [all_by_exchange(): blocks = lax.all_to_all(blocks, mesh_axis, split_axis=0, concat_axis=0)]
    all_gather x1 -> x0, waiting for transfers between devices: 145 us -> none  [per_device(): lax.all_gather(grad_matrix, 'seq', axis=0, tiled=True)]
  transfers between devices with their start and end apart: 11 -> 10, of which waited for: 7 -> 6; matrix products, arithmetic and copies ran while one was open for 2% -> 2% of each run, Pallas kernels for 0% -> 0%
where the time goes in v1:
time: 389 us; the launch traced here: 388 us
  blocking collectives  197 us (51%)
  waiting for transfers between devices  121 us (31%)
  starting transfers between devices  32.2 us (8%)
  between operations  13.9 us (4%)
  matrix products  12 us (3%)
  local copies, waits for them, and re-layouts  8.28 us (2%)
    all_to_all x1, blocking collectives, all_by_exchange(): blocks = lax.all_to_all(blocks, mesh_axis, split_axis=0, concat_axis=0)  197 us
    ppermute x1, waiting for transfers between devices, passed_along(): return lax.ppermute(block, axis, route)  59.4 us
    ppermute x8, waiting for transfers between devices, from_behind(): return lax.ppermute(shard, axis, pairs)  38.2 us
    reduce_scatter x1, waiting for transfers between devices, per_device(): lax.psum_scatter(partial_grad, 'mp', scatter_dimension=1, tiled=True)  23.5 us
    ppermute x8, starting transfers between devices, from_behind(): return lax.ppermute(shard, axis, pairs)  21.6 us
    ppermute x1, starting transfers between devices, passed_along(): return lax.ppermute(block, axis, route)  10.5 us
  transfers between devices with their start and end apart: 10, of which 6 were waited for; matrix products, arithmetic and copies ran while one was open for 2% of the time, Pallas kernels for 0%

profile of v1, /device:TPU:8, one launch (start us, length us, event | category | flops | bytes accessed | tf_op | source)
XLA Modules:
  0.0 388.4 jit_solution(7268377879816939848)
XLA Ops:
  6.5 1.1 copy.61
  7.6 1.0 copy.62
  8.7 3.5 collective-permute-start.3
  12.2 4.2 %collective-permute-start.2 = (bf16[128,1024]{0,1:T(8,128)(2,1)S(1)}, bf16[128,1024]{0,1:T(8,128)(2,1)S(1)}, u32[]{:S(2)}, u32[]{:S(2)}) collective-permute-start(bf16[128,1024]{0,1:T(8,128)(2,1)S(1)} %pad_maximum_fusion.5), channel_id=1, source_target_pairs={{0,4},{2,6},{4,8},{6,10},{8,12},{10,14},{12,16},{14,18},{16,20},{1... | collective-permute-start | bytes 786440 | tf_op jit(solution)/shard_map/ppermute | solution.py:22
  16.4 4.3 %collective-permute-start.1 = (bf16[128,1024]{0,1:T(8,128)(2,1)S(1)}, bf16[128,1024]{0,1:T(8,128)(2,1)S(1)}, u32[]{:S(2)}, u32[]{:S(2)}) collective-permute-start(bf16[128,1024]{0,1:T(8,128)(2,1)S(1)} %pad_maximum_fusion.5), channel_id=1, source_target_pairs={{0,6},{2,8},{4,10},{6,12},{8,14},{10,16},{12,18},{14,20},{16,22},{... | collective-permute-start | bytes 786440 | tf_op jit(solution)/shard_map/ppermute | solution.py:22
  20.7 3.8 collective-permute-start
  24.6 0.7 dynamic-slice_bitcast_fusion
  25.2 0.8 pad_dynamic-slice_fusion
  26.0 0.2 fusion.63
  26.3 0.9 reshape_squeeze.13
  27.2 0.9 reshape_squeeze.15
  28.1 0.1 copy.146
  28.3 1.1 copy.191
  29.4 0.2 copy.73
  29.6 0.3 fusion.77
  29.9 1.5 collective-permute-done
  31.4 0.3 fusion.80
  31.7 0.3 fusion.81
  32.0 0.3 fusion.79
  32.4 0.3 fusion.78
  32.7 0.5 fusion.55
  33.2 0.5 fusion.67
  33.7 0.2 fusion.91
  33.9 0.2 fusion.82
  34.1 0.2 fusion.90
  34.3 0.2 fusion.83
  34.6 0.2 fusion.89
  34.8 0.2 fusion.84
  35.0 0.2 fusion.88
  35.2 0.3 convolution_bitcast_fusion.1
  35.5 0.3 fusion.42
  35.8 0.3 fusion.39
  36.1 0.3 fusion.38
  36.4 0.3 fusion.37
  36.7 0.2 fusion.36
  36.9 0.3 fusion.40
  37.2 0.2 fusion.92
  37.4 0.2 fusion.44
  37.7 0.2 fusion.87
  37.9 0.2 fusion.46
  38.1 0.2 fusion.85
  38.3 0.2 fusion.45
  38.6 0.2 fusion.86
  38.8 0.2 fusion.47
  39.0 0.2 convolution_bitcast_fusion
  39.3 1.3 collective-permute-start.5
  40.6 1.3 collective-permute-start.6
  42.0 1.9 collective-permute-start.4
  44.0 1.3 collective-permute-start.7
  45.3 0.2 fusion.43
  45.5 0.3 fusion.41
  45.8 13.9 %collective-permute-done.5 = f32[128,1024]{0,1:T(8,128)S(1)} collective-permute-done((f32[128,1024]{0,1:T(8,128)S(1)}, f32[128,1024]{0,1:T(8,128)S(1)}, u32[]{:S(2)}, u32[]{:S(2)}) %collective-permute-start.5) | collective-permute-done | bytes 524320 | tf_op jit(solution)/shard_map/ppermute | solution.py:22
  59.7 14.0 %collective-permute-done.6 = f32[128,1024]{0,1:T(8,128)S(1)} collective-permute-done((f32[128,1024]{0,1:T(8,128)S(1)}, f32[128,1024]{0,1:T(8,128)S(1)}, u32[]{:S(2)}, u32[]{:S(2)}) %collective-permute-start.6) | collective-permute-done | bytes 524320 | tf_op jit(solution)/shard_map/ppermute | solution.py:22
  73.7 8.8 %collective-permute-done.7 = f32[128,1024]{0,1:T(8,128)S(1)} collective-permute-done((f32[128,1024]{0,1:T(8,128)S(1)}, f32[128,1024]{0,1:T(8,128)S(1)}, u32[]{:S(2)}, u32[]{:S(2)}) %collective-permute-start.7) | collective-permute-done | bytes 524320 | tf_op jit(solution)/shard_map/ppermute | solution.py:22
  82.5 0.1 fusion.51
  82.7 0.2 copy.111
  82.9 1.1 stack.2
  84.0 197.2 %all_to_all.5 = bf16[16,128,2048]{2,1,0:T(8,128)(2,1)S(1)} all-to-all(bf16[16,128,2048]{2,1,0:T(8,128)(2,1)S(1)} %stack.2), channel_id=1, replica_groups=mesh['section'=16,'seq'=16,'mp'=2] {'seq'}, dimensions={0} | all-to-all | bytes 16777216 | tf_op jit(solution)/shard_map/all_to_all | solution.py:15
  281.2 4.6 %fusion = f32[2048,336]{0,1:T(8,128)} fusion(bf16[2048,2048]{1,0:T(8,128)(2,1)S(1)} %bitcast.324, bf16[336,512]{1,0:T(8,128)(2,1)S(1)} %bitcast.388, bf16[336,512]{1,0:T(8,128)(2,1)S(1)} %bitcast.389, bf16[336,1024]{1,0:T(8,128)(2,1)S(1)} %bitcast.387), kind=kOutput, calls=%fused_computation | convolution fusion | flops 2822701056 | bytes 12517376 | tf_op jit(solution)/shard_map/dot_general | solution.py:186
  285.8 23.5 %reduce-scatter.2.cloned.1.call-done = f32[2048,168]{0,1:T(8,128)} async-done(((f32[2048,336]{0,1:T(8,128)}), f32[2048,168]{0,1:T(8,128)}) %reduce-scatter.2.cloned.1.call-update) | async-done | bytes 1376272 | tf_op jit(solution)/shard_map/reduce_scatter | solution.py:192
  309.4 1.4 convert_element_type.55
  310.8 10.5 %collective-permute-start.8 = (bf16[2048,168]{0,1:T(8,128)(2,1)S(1)}, bf16[2048,168]{0,1:T(8,128)(2,1)S(1)}, u32[]{:S(2)}, u32[]{:S(2)}) collective-permute-start(bf16[2048,168]{0,1:T(8,128)(2,1)S(1)} %convert_element_type.55), channel_id=1, source_target_pairs={{32,0},{64,32},{96,64},{128,96},{160,128},{192,160},{224,192},{256... | collective-permute-start | bytes 2064392 | tf_op jit(solution)/shard_map/ppermute | solution.py:28
  321.3 59.4 %collective-permute-done.8 = bf16[2048,168]{0,1:T(8,128)(2,1)S(1)} collective-permute-done((bf16[2048,168]{0,1:T(8,128)(2,1)S(1)}, bf16[2048,168]{0,1:T(8,128)(2,1)S(1)}, u32[]{:S(2)}, u32[]{:S(2)}) %collective-permute-start.8) | collective-permute-done | bytes 688160 | tf_op jit(solution)/shard_map/ppermute | solution.py:28
  380.7 0.8 copy.197
  (28 shorter events, 0.4 us)
Async XLA Ops:
  6.5 22.9 %copy-start = (bf16[1,128,1024]{2,1,0:T(8,128)(2,1)S(1)}, bf16[1,128,1024]{2,1,0:T(8,128)(2,1)}, u32[]{:S(2)}) copy-start(bf16[1,128,1024]{2,1,0:T(8,128)(2,1)} %param.11) | copy-start | bytes 786436
  6.5 302.8 %reduce-scatter.2.cloned.1.call-start = ((), (), s32[]{:S(2)}) async-start(), calls=%async_computation.2 | async-start | bytes 4128768 | tf_op jit(solution)/shard_map/reduce_scatter | solution.py:192
  8.7 23.7 %collective-permute-start.3 = (bf16[128,1024]{0,1:T(8,128)(2,1)S(1)}, bf16[128,1024]{0,1:T(8,128)(2,1)S(1)}, u32[]{:S(2)}, u32[]{:S(2)}) collective-permute-start(bf16[128,1024]{0,1:T(8,128)(2,1)S(1)} %pad_maximum_fusion.5), channel_id=1, source_target_pairs={{0,2},{2,4},{4,6},{6,8},{8,10},{10,12},{12,14},{14,16},{16,18},{18... | collective-permute-start | bytes 786440 | tf_op jit(solution)/shard_map/ppermute | solution.py:22
  12.2 19.8 %collective-permute-start.2 = (bf16[128,1024]{0,1:T(8,128)(2,1)S(1)}, bf16[128,1024]{0,1:T(8,128)(2,1)S(1)}, u32[]{:S(2)}, u32[]{:S(2)}) collective-permute-start(bf16[128,1024]{0,1:T(8,128)(2,1)S(1)} %pad_maximum_fusion.5), channel_id=1, source_target_pairs={{0,4},{2,6},{4,8},{6,10},{8,12},{10,14},{12,16},{14,18},{16,20},{1... | collective-permute-start | bytes 786440 | tf_op jit(solution)/shard_map/ppermute | solution.py:22
  16.4 15.3 %collective-permute-start.1 = (bf16[128,1024]{0,1:T(8,128)(2,1)S(1)}, bf16[128,1024]{0,1:T(8,128)(2,1)S(1)}, u32[]{:S(2)}, u32[]{:S(2)}) collective-permute-start(bf16[128,1024]{0,1:T(8,128)(2,1)S(1)} %pad_maximum_fusion.5), channel_id=1, source_target_pairs={{0,6},{2,8},{4,10},{6,12},{8,14},{10,16},{12,18},{14,20},{16,22},{... | collective-permute-start | bytes 786440 | tf_op jit(solution)/shard_map/ppermute | solution.py:22
  20.7 10.6 %collective-permute-start = (bf16[128,1024]{0,1:T(8,128)(2,1)S(1)}, bf16[128,1024]{0,1:T(8,128)(2,1)S(1)}, u32[]{:S(2)}, u32[]{:S(2)}) collective-permute-start(bf16[128,1024]{0,1:T(8,128)(2,1)S(1)} %pad_maximum_fusion.5), channel_id=1, source_target_pairs={{0,8},{2,10},{4,12},{6,14},{8,16},{10,18},{12,20},{14,22},{16,24},... | collective-permute-start | bytes 786440 | tf_op jit(solution)/shard_map/ppermute | solution.py:22
  39.3 20.4 %collective-permute-start.5 = (f32[128,1024]{0,1:T(8,128)S(1)}, f32[128,1024]{0,1:T(8,128)S(1)}, u32[]{:S(2)}, u32[]{:S(2)}) collective-permute-start(f32[128,1024]{0,1:T(8,128)S(1)} %pad_maximum_fusion.1), channel_id=1, source_target_pairs={{4,0},{6,2},{8,4},{10,6},{12,8},{14,10},{16,12},{18,14},{20,16},{2... | collective-permute-start | bytes 1572872 | tf_op jit(solution)/shard_map/ppermute | solution.py:22
  40.6 33.0 %collective-permute-start.6 = (f32[128,1024]{0,1:T(8,128)S(1)}, f32[128,1024]{0,1:T(8,128)S(1)}, u32[]{:S(2)}, u32[]{:S(2)}) collective-permute-start(f32[128,1024]{0,1:T(8,128)S(1)} %pad_maximum_fusion.2), channel_id=1, source_target_pairs={{6,0},{8,2},{10,4},{12,6},{14,8},{16,10},{18,12},{20,14},{22,16},{... | collective-permute-start | bytes 1572872 | tf_op jit(solution)/shard_map/ppermute | solution.py:22
  42.0 31.7 %collective-permute-start.4 = (f32[128,1024]{0,1:T(8,128)S(1)}, f32[128,1024]{0,1:T(8,128)S(1)}, u32[]{:S(2)}, u32[]{:S(2)}) collective-permute-start(f32[128,1024]{0,1:T(8,128)S(1)} %pad_maximum_fusion), channel_id=1, source_target_pairs={{2,0},{4,2},{6,4},{8,6},{10,8},{12,10},{14,12},{16,14},{18,16},{20... | collective-permute-start | bytes 1572872 | tf_op jit(solution)/shard_map/ppermute | solution.py:22
  44.0 38.6 %collective-permute-start.7 = (f32[128,1024]{0,1:T(8,128)S(1)}, f32[128,1024]{0,1:T(8,128)S(1)}, u32[]{:S(2)}, u32[]{:S(2)}) collective-permute-start(f32[128,1024]{0,1:T(8,128)S(1)} %pad_maximum_fusion.3), channel_id=1, source_target_pairs={{8,0},{10,2},{12,4},{14,6},{16,8},{18,10},{20,12},{22,14},{24,16},... | collective-permute-start | bytes 1572872 | tf_op jit(solution)/shard_map/ppermute | solution.py:22
  84.0 197.2 %copy-start.1 = (bf16[1,336,1024]{2,1,0:T(8,128)(2,1)S(1)}, bf16[1,336,1024]{2,1,0:T(8,128)(2,1)}, u32[]{:S(2)}) copy-start(bf16[1,336,1024]{2,1,0:T(8,128)(2,1)} %param.12) | copy-start | bytes 2064388
  84.0 197.2 %copy-start.2 = (bf16[1,336,512]{2,1,0:T(8,128)(2,1)S(1)}, bf16[1,336,512]{2,1,0:T(8,128)(2,1)}, u32[]{:S(2)}) copy-start(bf16[1,336,512]{2,1,0:T(8,128)(2,1)} %param.14) | copy-start | bytes 1032196
  84.0 197.2 %copy-start.3 = (bf16[1,336,512]{2,1,0:T(8,128)(2,1)S(1)}, bf16[1,336,512]{2,1,0:T(8,128)(2,1)}, u32[]{:S(2)}) copy-start(bf16[1,336,512]{2,1,0:T(8,128)(2,1)} %param.13) | copy-start | bytes 1032196
  310.8 69.9 %collective-permute-start.8 = (bf16[2048,168]{0,1:T(8,128)(2,1)S(1)}, bf16[2048,168]{0,1:T(8,128)(2,1)S(1)}, u32[]{:S(2)}, u32[]{:S(2)}) collective-permute-start(bf16[2048,168]{0,1:T(8,128)(2,1)S(1)} %convert_element_type.55), channel_id=1, source_target_pairs={{32,0},{64,32},{96,64},{128,96},{160,128},{192,160},{224,192},{256... | collective-permute-start | bytes 2064392 | tf_op jit(solution)/shard_map/ppermute | solution.py:28
Sparse Core Ops, SparseCore 0:
  286.0 23.3 reduce-scatter.1
